TPU v7x, 256 devices: a whole 4x4x8 slice. The times are simulated.
256 devices in a mesh: seg: 4 (over x), pair: 64 (over z, y, core).
Axes of the slice: x: 4, y: 4, z: 8, core: 2. Of those that a mesh axis runs over, the one named last changes fastest.
Arguments:
- traces: bfloat16 [4, 4096, 640], P('seg', 'pair'), may hold values from -160 to 160
- station_slot: int32 [64, 64], P('pair'), may hold values from 0 to 63, each once within a row
- block_pairs: int32 [256, 2], P('pair'), may hold values from 0 to 127, as said below
- pair_count: int32 [64], P('pair'), may hold values from 2 to 4
Outputs:
- correlations: bfloat16 [256, 1281, 1024], P('pair', None, 'seg')
Inputs may be any that keep to these rules, and one draw needn't show every extreme that they name: `block_pairs`: rows 4 o to 4 o + 3 belong to owner o. The first block of each row is one of o's own blocks 2 o to 2 o + 1; the second differs from the first and lies on device o - 1, o or o + 1; of the blocks of device o - 1, and of those of device o + 1, at most one is named in owner o's rows; the first row of each owner names a block of o - 1 and the second a block of o + 1 where those devices exist.
All inputs are finite; a program needn't handle non-finite values.
Results may differ from a plain program's by a relative error of at most 0.012.
The roundings to bfloat16 on the way count: a program that leaves them out, or rounds other values in their place, can miss the bound.
Values may be sent and summed in bfloat16 or wider, within the bound.
No kernel may reach another device: no remote copies, remote signals or barrier semaphores. Data moves between devices by JAX's collectives and lax.ppermute only.
A program may use at most 128 MiB of HBM per device.

v0:
```python
import math

import jax
import jax.numpy as jnp
from jax import lax
from jax.sharding import PartitionSpec as P

HALF_BAND = 64
BLK = 32


def passed_along(block, axis, distance):
    devices = range(lax.axis_size(axis))
    route = [(i - distance, i) for i in devices if i - distance in devices]
    return lax.ppermute(block, axis, route)


def forward_table(samples):
    sample_index = jnp.arange(samples, dtype=jnp.int32)
    phase_index = jnp.mod(sample_index[:, None] * sample_index[None, :], 2 * samples)
    angles = phase_index.astype(jnp.float32) * (math.pi / samples)
    return jnp.concatenate(
        [jnp.cos(angles).astype(jnp.bfloat16), (-jnp.sin(angles)).astype(jnp.bfloat16)], axis=1
    )


def inverse_table(samples):
    freq_bins = jnp.arange(samples, dtype=jnp.int32)
    shifts = jnp.arange(2 * samples + 1, dtype=jnp.int32) - samples
    phase_index = jnp.mod(shifts[:, None] * freq_bins[None, :], 2 * samples)
    angles = phase_index.astype(jnp.float32) * (math.pi / samples)
    weight = jnp.where(freq_bins == 0, 1.0, 2.0).astype(jnp.float32)[None, :]
    return jnp.concatenate(
        [
            (weight * jnp.cos(angles)).astype(jnp.bfloat16),
            (-weight * jnp.sin(angles)).astype(jnp.bfloat16),
        ],
        axis=1,
    )


def whiten(series, half_band):
    samples = series.shape[1]
    spectra = jnp.dot(series, forward_table(samples), preferred_element_type=jnp.float32)
    real_part = spectra[:, :samples]
    imag_part = spectra[:, samples:]
    powers = real_part * real_part + imag_part * imag_part
    freq_bins = jnp.arange(samples, dtype=jnp.int32)
    window = (jnp.abs(freq_bins[:, None] - freq_bins[None, :]) <= half_band).astype(jnp.float32)
    counts = jnp.sum(window, axis=0)
    smooth = jnp.dot(powers, window, precision=lax.Precision.HIGHEST) / counts[None, :]
    factor = lax.rsqrt(smooth + 1e-06)
    return (spectra * jnp.concatenate([factor, factor], axis=1)).astype(jnp.bfloat16)


def cross_spectra(first_rows, second_rows):
    slot_total = first_rows.shape[1]
    bin_count = first_rows.shape[3] // 2
    first_real = first_rows[..., :bin_count]
    first_imag = first_rows[..., bin_count:]
    second_real = second_rows[..., :bin_count]
    second_imag = second_rows[..., bin_count:]

    def product(left_part, right_part):
        return jnp.einsum(
            "szif,szjf->zfij", left_part, right_part, preferred_element_type=jnp.float32
        )

    real_sum = product(first_real, second_real) + product(first_imag, second_imag)
    imag_sum = product(first_imag, second_real) - product(first_real, second_imag)
    return jnp.concatenate(
        [real_sum.reshape(slot_total, bin_count, -1), imag_sum.reshape(slot_total, bin_count, -1)],
        axis=1,
    )


def body(traces, station_slot, block_pairs, pair_count):
    seg_dev, sta_dev, samples = traces.shape
    white = whiten(traces.reshape(seg_dev * sta_dev, samples), HALF_BAND).reshape(
        seg_dev, sta_dev, 2 * samples
    )
    ordered = jnp.zeros_like(white).at[:, station_slot[0], :].set(white)
    source = lax.all_gather(ordered, "seg", axis=0, tiled=True)
    owner_index = lax.axis_index("pair")
    per_device = sta_dev // BLK
    block_ids = block_pairs - per_device * owner_index
    shard_before = passed_along(source, "pair", 1)
    shard_after = passed_along(source, "pair", -1)
    candidates = jnp.concatenate([shard_before, source, shard_after], axis=1)
    local_block = block_ids + per_device
    seg_index = lax.axis_index("seg")
    quarter = BLK // lax.axis_size("seg")
    first_index = (
        local_block[:, 0:1] * BLK
        + seg_index * quarter
        + jnp.arange(quarter, dtype=jnp.int32)[None, :]
    )
    second_index = local_block[:, 1:2] * BLK + jnp.arange(BLK, dtype=jnp.int32)[None, :]
    first_rows = jnp.take(candidates, first_index, axis=1)
    second_rows = jnp.take(candidates, second_index, axis=1)
    stacked = cross_spectra(first_rows, second_rows).astype(jnp.bfloat16)
    inverse = inverse_table(samples)
    norm_scale = 1.0 / math.sqrt(2.0 * samples * candidates.shape[0])
    slot_total = block_pairs.shape[0]
    live_mask = jnp.arange(slot_total, dtype=jnp.int32) < pair_count[0]
    correlated = (
        jnp.einsum("lk,zkp->zlp", inverse, stacked, preferred_element_type=jnp.float32) * norm_scale
    )
    return jnp.where(live_mask[:, None, None], correlated, 0.0).astype(jnp.bfloat16)


def solution(mesh):
    return jax.shard_map(
        body,
        mesh=mesh,
        in_specs=(P("seg", "pair", None), P("pair", None), P("pair", None), P("pair")),
        out_specs=P("pair", None, "seg"),
        check_vma=False,
    )
```

profile of v0, /device:TPU:128, one launch (start us, length us, event | category | flops | bytes accessed | tf_op | source)
XLA Modules:
  0.0 138.6 jit_solution(4644614725696383619)
XLA Ops:
  0.0 7.0 %negate_convert_fusion = (bf16[640,640]{1,0:T(8,128)(2,1)S(1)}, bf16[640,640]{1,0:T(8,128)(2,1)S(1)}) fusion(), kind=kLoop, calls=%fused_computation.45 | loop fusion | flops 4915200 | bytes 1638400 | tf_op jit(solution)/shard_map/convert_element_type | solution.py:23
  9.6 13.4 %all-gather = bf16[256,1280]{1,0:T(8,128)(2,1)S(1)} all-gather(bf16[64,1280]{1,0:T(8,128)(2,1)S(1)} %scatter_custom_fusion), channel_id=2, replica_groups=mesh['seg'=4,'pair'=64] {'seg'}, dimensions={0}, use_global_device_ids=true | all-gather | bytes 819200 | tf_op jit(solution)/shard_map/all_gather | solution.py:83
  23.5 1.9 %collective-permute-start = (bf16[4,64,1280]{2,0,1:T(4,128)(2,1)S(1)}, bf16[4,64,1280]{2,0,1:T(4,128)(2,1)}, u32[]{:S(2)}, u32[]{:S(2)}) collective-permute-start(bf16[4,64,1280]{2,0,1:T(4,128)(2,1)S(1)} %copy.18), channel_id=1, source_target_pairs={{0,1},{1,2},{2,3},{3,4},{4,5},{5,6},{6,7},{7,8},{8,9},{9,10},{10,1... | collective-permute-start | bytes 1966088 | tf_op jit(solution)/shard_map/ppermute | solution.py:15
  25.5 7.1 %collective-permute-start.1 = (bf16[4,64,1280]{2,0,1:T(4,128)(2,1)S(1)}, bf16[4,64,1280]{2,0,1:T(4,128)(2,1)}, u32[]{:S(2)}, u32[]{:S(2)}) collective-permute-start(bf16[4,64,1280]{2,0,1:T(4,128)(2,1)S(1)} %copy.18), channel_id=1, source_target_pairs={{1,0},{2,1},{3,2},{4,3},{5,4},{6,5},{7,6},{8,7},{9,8},{10,9},{11,1... | collective-permute-start | bytes 1966088 | tf_op jit(solution)/shard_map/ppermute | solution.py:15
  34.3 15.3 %multiply_convert_fusion.1 = (bf16[1281,640]{1,0:T(8,128)(2,1)}, bf16[1281,640]{1,0:T(8,128)(2,1)}) fusion(s32[1281]{0:T(1024)S(1)} %iota_add_fusion, f32[640]{0:T(1024)S(1)} %get-tuple-element.9, f32[640]{0:T(1024)S(1)} %get-tuple-element.10), kind=kLoop, calls=%fused_computation.23 | loop fusion | flops 10657920 | bytes 3289604 | tf_op jit(solution)/shard_map/convert_element_type | solution.py:35
  52.9 1.7 %gather_fusion.1 = bf16[128,4,1280]{2,1,0:T(4,128)(2,1)S(1)} fusion(bf16[4,192,1280]{2,0,1:T(4,128)(2,1)S(1)} %constant_dynamic-update-slice_fusion, s32[1024]{0:T(1024)S(1)} %get-tuple-element.13), kind=kCustom, calls=%fused_computation.1 | custom fusion | bytes 2621952 | tf_op jit(solution)/shard_map/jit(_take)/gather | solution.py:100
  54.6 5.9 %copy.24 = bf16[4,32,4,1280]{1,2,3,0:T(4,128)(2,1)} copy(bf16[4,32,4,1280]{3,2,1,0:T(4,128)(2,1)S(1)} %bitcast.66) | data formatting | bytes 2621440 | tf_op jit(solution)/shard_map/jit(_take)/gather | solution.py:100
  60.4 5.1 %select_bitcast_fusion = bf16[4,4,32,1280]{2,0,3,1:T(4,128)(2,1)S(1)} fusion(bf16[4,32,4,1280]{1,2,3,0:T(4,128)(2,1)} %copy.24, pred[4,32]{1,0:T(4,128)(4,1)S(1)} %fusion.53), kind=kLoop, calls=%fused_computation.14 | loop fusion | flops 655360 | bytes 2621568 | tf_op jit(solution)/shard_map/jit(_take)/select_n | solution.py:100
  65.6 2.4 %fusion.91 = bf16[4,4,32,640]{2,0,3,1:T(4,128)(2,1)} fusion(bf16[4,4,32,1280]{2,0,3,1:T(4,128)(2,1)S(1)} %select_bitcast_fusion), kind=kLoop, calls=%fused_computation.35.clone.2 | loop fusion | bytes 1310720 | tf_op jit(solution)/shard_map/szif,szjf->zfij/dot_general | solution.py:65
  67.9 2.4 %fusion.89 = bf16[4,4,32,640]{2,0,3,1:T(4,128)(2,1)} fusion(bf16[4,4,32,1280]{2,0,3,1:T(4,128)(2,1)S(1)} %select_bitcast_fusion), kind=kLoop, calls=%fused_computation.37.clone.2 | loop fusion | bytes 1310720 | tf_op jit(solution)/shard_map/szif,szjf->zfij/dot_general | solution.py:65
  70.3 2.4 %fusion.93 = bf16[4,4,32,640]{2,0,3,1:T(4,128)(2,1)} fusion(bf16[4,4,32,1280]{2,0,3,1:T(4,128)(2,1)S(1)} %select_bitcast_fusion), kind=kLoop, calls=%fused_computation.36.clone.2 | loop fusion | bytes 1310720 | tf_op jit(solution)/shard_map/szif,szjf->zfij/dot_general | solution.py:65
  72.7 2.4 %fusion.87 = bf16[4,4,32,640]{2,0,3,1:T(4,128)(2,1)} fusion(bf16[4,4,32,1280]{2,0,3,1:T(4,128)(2,1)S(1)} %select_bitcast_fusion), kind=kLoop, calls=%fused_computation.34.clone.2 | loop fusion | bytes 1310720 | tf_op jit(solution)/shard_map/szif,szjf->zfij/dot_general | solution.py:65
  75.2 1.5 %gather_fusion = bf16[32,4,1280]{2,1,0:T(4,128)(2,1)} fusion(bf16[4,192,1280]{2,0,1:T(4,128)(2,1)S(1)} %constant_dynamic-update-slice_fusion, s32[1024]{0:T(1024)S(1)} %get-tuple-element.14), kind=kCustom, calls=%fused_computation | custom fusion | bytes 655488 | tf_op jit(solution)/shard_map/jit(_take)/gather | solution.py:99
  76.7 7.1 %copy.22 = bf16[4,8,4,1280]{1,2,3,0:T(4,128)(2,1)} copy(bf16[4,8,4,1280]{3,2,1,0:T(4,128)(2,1)} %bitcast.67) | data formatting | bytes 655360 | tf_op jit(solution)/shard_map/jit(_take)/gather | solution.py:99
  83.7 7.3 %fusion = f32[4,640,8,32]{3,2,1,0:T(8,128)} fusion(bf16[4,8,4,1280]{1,2,3,0:T(4,128)(2,1)} %copy.22, pred[4,8]{1,0:T(4,128)(4,1)S(1)} %fusion.52, bf16[4,4,32,640]{2,0,3,1:T(4,128)(2,1)S(1)} %copy-done.6), kind=kOutput, calls=%fused_computation.6 | convolution fusion | flops 5406720 | bytes 3604512 | tf_op jit(solution)/shard_map/szif,szjf->zfij/dot_general | solution.py:65
  91.1 8.9 %add_convert_fusion = bf16[4,640,8,32]{3,2,1,0:T(8,128)(2,1)} fusion(f32[4,640,8,32]{3,2,1,0:T(8,128)} %fusion, bf16[4,8,4,1280]{1,2,3,0:T(4,128)(2,1)S(1)} %copy-done.2, pred[4,8]{1,0:T(4,128)(4,1)S(1)} %fusion.52, bf16[4,4,32,640]{2,0,3,1:T(4,128)(2,1)S(1)} %copy-done.5), kind=kOutput, calls=%fused_computation.4 | convolution fusion | flops 6717440 | bytes 4915232 | tf_op jit(solution)/shard_map/szif,szjf->zfij/dot_general | solution.py:65
  100.0 5.2 %copy.25 = bf16[4,640,8,32]{1,3,2,0:T(8,128)(2,1)S(1)} copy(bf16[4,640,8,32]{3,2,1,0:T(8,128)(2,1)} %add_convert_fusion) | data formatting | bytes 2621440 | tf_op jit(solution)/shard_map/convert.3
  105.1 1.5 %copy.27 = bf16[4,640,256]{2,1,0:T(8,128)(2,1)} copy(bf16[4,640,256]{1,2,0:T(8,128)(2,1)S(1)} %bitcast.64) | data formatting | bytes 2621440 | tf_op jit(solution)/shard_map/reshape | solution.py:72
  106.6 5.4 %fusion.4 = f32[4,640,8,32]{3,2,1,0:T(8,128)S(1)} fusion(bf16[4,8,4,1280]{1,2,3,0:T(4,128)(2,1)} %copy.22, pred[4,8]{1,0:T(4,128)(4,1)S(1)} %fusion.52, bf16[4,4,32,640]{2,0,3,1:T(4,128)(2,1)} %fusion.93), kind=kOutput, calls=%fused_computation.10 | convolution fusion | flops 5406720 | bytes 3604512 | tf_op jit(solution)/shard_map/szif,szjf->zfij/dot_general | solution.py:65
  112.0 5.3 %subtract_convert_fusion = bf16[4,640,8,32]{3,2,1,0:T(8,128)(2,1)} fusion(f32[4,640,8,32]{3,2,1,0:T(8,128)S(1)} %fusion.4, bf16[4,8,4,1280]{1,2,3,0:T(4,128)(2,1)S(1)} %copy-done.3, pred[4,8]{1,0:T(4,128)(4,1)S(1)} %fusion.52, bf16[4,4,32,640]{2,0,3,1:T(4,128)(2,1)S(1)} %copy-done.4), kind=kOutput, calls=%fused_computation.3 | convolution fusion | flops 6717440 | bytes 4915232 | tf_op jit(solution)/shard_map/szif,szjf->zfij/dot_general | solution.py:65
  117.3 5.2 %copy.26 = bf16[4,640,8,32]{1,3,2,0:T(8,128)(2,1)S(1)} copy(bf16[4,640,8,32]{3,2,1,0:T(8,128)(2,1)} %subtract_convert_fusion) | data formatting | bytes 2621440 | tf_op jit(solution)/shard_map/convert.2
  122.5 1.5 %copy.28 = bf16[4,640,256]{2,1,0:T(8,128)(2,1)} copy(bf16[4,640,256]{1,2,0:T(8,128)(2,1)S(1)} %bitcast.65) | data formatting | bytes 2621440 | tf_op jit(solution)/shard_map/reshape | solution.py:72
  124.2 6.0 %fusion.15 = bf16[4,1281,256]{2,1,0:T(8,128)(2,1)S(1)} fusion(bf16[1281,640]{1,0:T(8,128)(2,1)} %get-tuple-element.6, bf16[1281,640]{1,0:T(8,128)(2,1)S(1)} %copy-done.7, pred[4]{0:T(512)(128)(4,1)S(1)} %copy-done.9, bf16[4,640,256]{2,1,0:T(8,128)(2,1)} %copy.28, bf16[4,640,256]{2,1,0:T(8,128)(2,1)} %copy.27), kind=kOutput, calls=%fused_computation.28 | convolution fusion | flops 3373801472 | bytes 8524292 | tf_op jit(solution)/shard_map/lk,zkp->zlp/dot_general | solution.py:107
  130.2 8.4 %copy.29 = bf16[4,1281,256]{2,0,1:T(4,128)(2,1)} copy(bf16[4,1281,256]{2,1,0:T(8,128)(2,1)S(1)} %fusion.15) | data formatting | bytes 5246976 | tf_op jit(solution)/shard_map/convert_element_type | solution.py:109
  (43 shorter events, 7.5 us)
Async XLA Ops:
  0.0 7.8 %copy-start = (bf16[1,64,640]{2,1,0:T(8,128)(2,1)S(1)}, bf16[1,64,640]{2,1,0:T(8,128)(2,1)}, u32[]{:S(2)}) copy-start(bf16[1,64,640]{2,1,0:T(8,128)(2,1)} %param.4) | copy-start | bytes 245764
  8.1 24.5 %copy-start.8 = (s32[4,2]{0,1:T(2,128)S(1)}, s32[4,2]{0,1:T(2,128)}, u32[]{:S(2)}) copy-start(s32[4,2]{0,1:T(2,128)} %param.6) | copy-start | bytes 100
  23.5 26.1 %collective-permute-start = (bf16[4,64,1280]{2,0,1:T(4,128)(2,1)S(1)}, bf16[4,64,1280]{2,0,1:T(4,128)(2,1)}, u32[]{:S(2)}, u32[]{:S(2)}) collective-permute-start(bf16[4,64,1280]{2,0,1:T(4,128)(2,1)S(1)} %copy.18), channel_id=1, source_target_pairs={{0,1},{1,2},{2,3},{3,4},{4,5},{5,6},{6,7},{7,8},{8,9},{9,10},{10,1... | collective-permute-start | bytes 1966088 | tf_op jit(solution)/shard_map/ppermute | solution.py:15
  25.5 26.0 %collective-permute-start.1 = (bf16[4,64,1280]{2,0,1:T(4,128)(2,1)S(1)}, bf16[4,64,1280]{2,0,1:T(4,128)(2,1)}, u32[]{:S(2)}, u32[]{:S(2)}) collective-permute-start(bf16[4,64,1280]{2,0,1:T(4,128)(2,1)S(1)} %copy.18), channel_id=1, source_target_pairs={{1,0},{2,1},{3,2},{4,3},{5,4},{6,5},{7,6},{8,7},{9,8},{10,9},{11,1... | collective-permute-start | bytes 1966088 | tf_op jit(solution)/shard_map/ppermute | solution.py:15
  76.7 7.1 %copy-start.6 = (bf16[4,4,32,640]{2,0,3,1:T(4,128)(2,1)S(1)}, bf16[4,4,32,640]{2,0,3,1:T(4,128)(2,1)}, u32[]{:S(2)}) copy-start(bf16[4,4,32,640]{2,0,3,1:T(4,128)(2,1)} %fusion.91) | copy-start | bytes 1966084
  83.7 7.3 %copy-start.2 = (bf16[4,8,4,1280]{1,2,3,0:T(4,128)(2,1)S(1)}, bf16[4,8,4,1280]{1,2,3,0:T(4,128)(2,1)}, u32[]{:S(2)}) copy-start(bf16[4,8,4,1280]{1,2,3,0:T(4,128)(2,1)} %copy.22) | copy-start | bytes 983044
  83.7 7.3 %copy-start.5 = (bf16[4,4,32,640]{2,0,3,1:T(4,128)(2,1)S(1)}, bf16[4,4,32,640]{2,0,3,1:T(4,128)(2,1)}, u32[]{:S(2)}) copy-start(bf16[4,4,32,640]{2,0,3,1:T(4,128)(2,1)} %fusion.89) | copy-start | bytes 1966084
  106.6 5.4 %copy-start.3 = (bf16[4,8,4,1280]{1,2,3,0:T(4,128)(2,1)S(1)}, bf16[4,8,4,1280]{1,2,3,0:T(4,128)(2,1)}, u32[]{:S(2)}) copy-start(bf16[4,8,4,1280]{1,2,3,0:T(4,128)(2,1)} %copy.22) | copy-start | bytes 983044
  106.6 5.4 %copy-start.4 = (bf16[4,4,32,640]{2,0,3,1:T(4,128)(2,1)S(1)}, bf16[4,4,32,640]{2,0,3,1:T(4,128)(2,1)}, u32[]{:S(2)}) copy-start(bf16[4,4,32,640]{2,0,3,1:T(4,128)(2,1)} %fusion.87) | copy-start | bytes 1966084
  122.5 1.6 %copy-start.7 = (bf16[1281,640]{1,0:T(8,128)(2,1)S(1)}, bf16[1281,640]{1,0:T(8,128)(2,1)}, u32[]{:S(2)}) copy-start(bf16[1281,640]{1,0:T(8,128)(2,1)} %get-tuple-element.5) | copy-start | bytes 4919044
  122.5 1.6 %copy-start.9 = (pred[4]{0:T(512)(128)(4,1)S(1)}, pred[4]{0:T(512)(128)(4,1)}, u32[]{:S(2)}) copy-start(pred[4]{0:T(512)(128)(4,1)} %iota_compare_fusion.1) | copy-start | bytes 16
  124.2 14.4 %copy-start.1 = (bf16[1,64,640]{2,1,0:T(8,128)(2,1)S(1)}, bf16[1,64,640]{2,1,0:T(8,128)(2,1)}, u32[]{:S(2)}) copy-start(bf16[1,64,640]{2,1,0:T(8,128)(2,1)} %param.4) | copy-start | bytes 245764
where the time goes:
time: 140 us; the launch traced here: 139 us
  local copies, waits for them, and re-layouts  51.6 us (37%)
  matrix products  33.8 us (24%)
  other arithmetic  29.9 us (21%)
  blocking collectives  13.4 us (10%)
  starting transfers between devices  9.07 us (6%)
    dot_general x4, matrix products, product(): jnp.einsum('szif,szjf->zfij', left_part, right_part, preferred_element_ty...  26.9 us
    convert_element_type x1, other arithmetic, inverse_table(): (weight * jnp.cos(angles)).astype(jnp.bfloat16)  15.3 us
    all_gather x1, blocking collectives, body(): source = lax.all_gather(ordered, 'seg', axis=0, tiled=True)  13.4 us
    another operation x2, local copies, waits for them, and re-layouts  10.4 us
    dot_general x4, local copies, waits for them, and re-layouts, product(): jnp.einsum('szif,szjf->zfij', left_part, right_part, preferred_element_ty...  9.59 us
    ppermute x2, starting transfers between devices, passed_along(): return lax.ppermute(block, axis, route)  9.07 us
    gather x2, local copies, waits for them, and re-layouts, body(): first_rows = jnp.take(candidates, first_index, axis=1)  8.58 us
    convert_element_type x1, local copies, waits for them, and re-layouts, body(): jnp.where(live_mask[:, None, None], correlated, 0.0).astype(jnp.bfloat16)  8.44 us
  transfers between devices with their start and end apart: 2, of which 0 were waited for; matrix products, arithmetic and copies ran while one was open for 13% of the time, Pallas kernels for 0%

commit v1 on v0

v1 whole, which is shorter than its diff:
```python
import functools
import math

import jax
import jax.numpy as jnp
import numpy as np
from jax import lax
from jax.experimental import pallas as pl
from jax.experimental.pallas import tpu as pltpu
from jax.sharding import Mesh
from jax.sharding import PartitionSpec as P

N = 640
HALF_BAND = 64
BLK = 32
SEG = 4
SLOTS = 4
LANES = 128
KB = N // LANES
ROWS = SEG * BLK
OUT_ROWS = (2 * N + 1) * 8
NT = (((1,), (1,)), ((), ()))
VMEM = pl.BlockSpec(memory_space=pltpu.VMEM)
SMEM = pl.BlockSpec(memory_space=pltpu.SMEM)
f32 = jnp.float32
bf16 = jnp.bfloat16


def bin_order():
    return np.concatenate([np.arange(0, N, 2), np.arange(1, N, 2)])


def fourier_table():
    bins = bin_order()
    phase = (np.arange(N)[:, None] * bins[None, :]) % (2 * N)
    angle = phase * (math.pi / N)
    real = np.cos(angle).reshape(N, KB, 1, LANES)
    imag = -np.sin(angle).reshape(N, KB, 1, LANES)
    return np.concatenate([real, imag], axis=2).reshape(N, 2 * N).astype(bf16)


def window_table():
    bins = bin_order()
    return (np.abs(bins[:, None] - bins[None, :]) <= HALF_BAND).astype(bf16)


def bin_rows():
    bins = bin_order()
    counts = np.minimum(bins, HALF_BAND) + np.minimum(N - 1 - bins, HALF_BAND) + 1
    weight = np.where(bins == 0, 0.5, 1.0)
    return np.stack([1.0 / counts, weight]).astype(np.float32)


def order_kernel(slot_ref, gathered_ref, blocks_ref):
    place = lax.broadcasted_iota(jnp.int32, (2 * BLK, 2 * BLK), 0)
    onehot = (place == slot_ref[...]).astype(bf16)
    for s in range(SEG):
        rows = jnp.dot(onehot, gathered_ref[s], preferred_element_type=f32).astype(bf16)
        blocks_ref[0, s * BLK : (s + 1) * BLK, :] = rows[:BLK]
        blocks_ref[1, s * BLK : (s + 1) * BLK, :] = rows[BLK:]


def order_rows(station_slot, gathered):
    return pl.pallas_call(
        order_kernel,
        out_shape=jax.ShapeDtypeStruct((2, ROWS, N), bf16),
        in_specs=[VMEM, VMEM],
        out_specs=VMEM,
        name="order_rows",
    )(station_slot, gathered)


def whiten_rows(rows, table_ref, window_ref, bins_ref, spec_ref, hi_ref, lo_ref, store):
    for kb in range(KB):
        cols = slice(2 * kb * LANES, 2 * (kb + 1) * LANES)
        lanes = slice(kb * LANES, (kb + 1) * LANES)
        spec = jnp.dot(rows, table_ref[:, cols], preferred_element_type=f32)
        spec_ref[:, cols] = spec
        real, imag = spec[:, :LANES], spec[:, LANES:]
        power = real * real + imag * imag
        high = power.astype(bf16)
        hi_ref[:, lanes] = high
        lo_ref[:, lanes] = (power - high.astype(f32)).astype(bf16)
    total = jnp.dot(hi_ref[...], window_ref[...], preferred_element_type=f32)
    total += jnp.dot(lo_ref[...], window_ref[...], preferred_element_type=f32)
    factor = lax.rsqrt(total * bins_ref[0:1, :] + 1e-06)
    for kb in range(KB):
        scale = factor[:, kb * LANES : (kb + 1) * LANES]
        for part in range(2):
            start = (2 * kb + part) * LANES
            cols = slice(start, start + LANES)
            store(cols, (spec_ref[:, cols] * scale).astype(bf16))


def own_kernel(blocks_ref, table_ref, window_ref, bins_ref, white_ref, spec_ref, hi_ref, lo_ref):
    rows = blocks_ref[...].reshape(2 * ROWS, N)

    def store(cols, value):
        white_ref[:, cols] = value.astype(f32)

    whiten_rows(rows, table_ref, window_ref, bins_ref, spec_ref, hi_ref, lo_ref, store)


def whiten_scratch():
    return [
        pltpu.VMEM((2 * ROWS, 2 * N), f32),
        pltpu.VMEM((2 * ROWS, N), bf16),
        pltpu.VMEM((2 * ROWS, N), bf16),
    ]


def whiten_own(blocks, table, window, bins):
    return pl.pallas_call(
        own_kernel,
        out_shape=jax.ShapeDtypeStruct((2 * ROWS, 2 * N), f32),
        in_specs=[VMEM] * 4,
        out_specs=VMEM,
        scratch_shapes=whiten_scratch(),
        name="whiten_own",
    )(blocks, table, window, bins)


def main_kernel(
    meta_ref,
    own_ref,
    mate_ref,
    far_ref,
    table_ref,
    window_ref,
    bins_ref,
    out_ref,
    white_ref,
    spec_ref,
    hi_ref,
    lo_ref,
    mid_ref,
    first_ref,
    cross_ref,
    lag_ref,
    low_ref,
    sems,
):
    owner, seg_index, count = meta_ref[9], meta_ref[10], meta_ref[8]
    mate = owner + 1 - 2 * (owner % 2)

    mate_pick, far_pick = 0, 0
    first_base, second_base = [], []
    for z in range(SLOTS):
        first, second = meta_ref[2 * z], meta_ref[2 * z + 1]
        device, half = second // 2, second % 2
        is_own, is_mate = device == owner, device == mate
        mate_pick = jnp.where(is_mate, half, mate_pick)
        far_pick = jnp.where(is_own | is_mate, far_pick, half)
        place = jnp.where(is_own, half, jnp.where(is_mate, 2, 3))
        second_base.append(place * ROWS)
        first_base.append((first % 2) * ROWS + seg_index * (BLK // SEG))

    white_ref[: 2 * ROWS, :] = own_ref[...]
    rows = jnp.concatenate([mate_ref[mate_pick], far_ref[far_pick]], axis=0)

    def store(cols, value):
        white_ref[2 * ROWS :, cols] = value.astype(f32)

    whiten_rows(rows, table_ref, window_ref, bins_ref, spec_ref, hi_ref, lo_ref, store)

    middle = table_ref[:, 2 * 2 * LANES : 2 * 3 * LANES]
    even = lax.broadcasted_iota(jnp.int32, (1, 2 * LANES), 1) % LANES < LANES // 2
    mid_ref[:, : 2 * LANES] = jnp.where(even, middle, jnp.zeros_like(middle))
    mid_ref[:, 2 * LANES :] = jnp.where(even, jnp.zeros_like(middle), middle)

    for z in range(SLOTS):
        for s in range(SEG):
            start = pl.multiple_of(first_base[z] + s * BLK, 8)
            first_ref[s * 8 : (s + 1) * 8, :] = white_ref[pl.ds(start, 8), :]

        def cross_step(kb, carry, z=z):
            real_col = pl.multiple_of(2 * kb * LANES, LANES)
            imag_col = pl.multiple_of((2 * kb + 1) * LANES, LANES)
            weight = bins_ref[1:2, pl.ds(pl.multiple_of(kb * LANES, LANES), LANES)]
            for half in range(2):
                second = []
                for s in range(SEG):
                    start = pl.multiple_of(second_base[z] + s * BLK + half * 16, 16)
                    second.append(
                        (
                            white_ref[pl.ds(start, 16), pl.ds(real_col, LANES)] * weight,
                            white_ref[pl.ds(start, 16), pl.ds(imag_col, LANES)] * weight,
                        )
                    )
                for i in range(BLK // SEG):
                    real, imag = 0.0, 0.0
                    for s in range(SEG):
                        row = slice(s * 8 + i, s * 8 + i + 1)
                        a_re = first_ref[row, pl.ds(real_col, LANES)]
                        a_im = first_ref[row, pl.ds(imag_col, LANES)]
                        b_re, b_im = second[s]
                        real = real + (a_re * b_re + a_im * b_im)
                        imag = imag + (a_im * b_re - a_re * b_im)
                    at = slice(i * BLK + half * 16, i * BLK + half * 16 + 16)
                    cross_ref[at, pl.ds(real_col, LANES)] = real.astype(bf16)
                    cross_ref[at, pl.ds(imag_col, LANES)] = imag.astype(bf16)
            return carry

        lax.fori_loop(0, KB, cross_step, 0)

        step = N // 2
        for half in range(2):
            at = slice(half * step, (half + 1) * step)
            low_side = lax.dot_general(
                table_ref[at, : 4 * LANES], cross_ref[:, : 4 * LANES], NT, preferred_element_type=f32
            ) + lax.dot_general(
                mid_ref[at, : 2 * LANES],
                cross_ref[:, 4 * LANES : 6 * LANES],
                NT,
                preferred_element_type=f32,
            )
            high_side = lax.dot_general(
                table_ref[at, 6 * LANES :], cross_ref[:, 6 * LANES :], NT, preferred_element_type=f32
            ) + lax.dot_general(
                mid_ref[at, 2 * LANES :],
                cross_ref[:, 4 * LANES : 6 * LANES],
                NT,
                preferred_element_type=f32,
            )
            minus, plus = low_side - high_side, low_side + high_side
            for ct in range(2):
                lanes = slice(ct * LANES, (ct + 1) * LANES)
                start = half * step * 8 + ct * 4 + z
                lag_ref[pl.ds(start, step, stride=8), :] = minus[:, lanes]
                lag_ref[pl.ds(start + N * 8, step, stride=8), :] = plus[:, lanes]

    slot = lax.broadcasted_iota(jnp.int32, (8, LANES), 0) % SLOTS
    scale = 2.0 / math.sqrt(2.0 * N * SEG)
    chunks = 8
    size = 2 * N * 8 // chunks
    copies = []
    for c in range(chunks):
        value = lag_ref[c * size : (c + 1) * size, :].reshape(size // 8, 8, LANES)
        value = jnp.where((slot < count)[None], value * scale, 0.0)
        low_ref[c * size : (c + 1) * size, :] = value.reshape(size, LANES).astype(bf16)
        copy = pltpu.make_async_copy(
            low_ref.at[pl.ds(c * size, size)], out_ref.at[pl.ds(c * size, size)], sems.at[c]
        )
        copy.start()
        copies.append(copy)
    last = pltpu.make_async_copy(
        low_ref.at[pl.ds(0, 8)], out_ref.at[pl.ds(2 * N * 8, 8)], sems.at[chunks]
    )
    last.start()
    for copy in copies:
        copy.wait()
    last.wait()


def correlate(meta, own_white, mate, far, table, window, bins):
    return pl.pallas_call(
        main_kernel,
        out_shape=jax.ShapeDtypeStruct((OUT_ROWS, LANES), bf16),
        in_specs=[SMEM] + [VMEM] * 6,
        out_specs=pl.BlockSpec(memory_space=pltpu.HBM),
        scratch_shapes=[pltpu.VMEM((4 * ROWS, 2 * N), f32)]
        + whiten_scratch()
        + [
            pltpu.VMEM((N, 4 * LANES), bf16),
            pltpu.VMEM((BLK, 2 * N), f32),
            pltpu.VMEM((2 * ROWS, 2 * N), bf16),
            pltpu.VMEM((2 * N * 8, LANES), f32),
            pltpu.VMEM((2 * N * 8, LANES), bf16),
            pltpu.SemaphoreType.DMA((9,)),
        ],
        name="correlate",
    )(meta, own_white, mate, far, table, window, bins)


def unpack(packed):
    lags = 2 * N + 1
    split = packed.reshape(lags, 2, SLOTS, LANES)
    return jnp.transpose(split, (2, 0, 1, 3)).reshape(SLOTS, lags, 2 * LANES)


def body(traces, station_slot, block_pairs, pair_count):
    pair = ("chip", "core")
    owners = lax.axis_size("chip") * 2
    table = jnp.asarray(fourier_table())
    window = jnp.asarray(window_table())
    bins = jnp.asarray(bin_rows())

    def along(distance):
        return [(i, (i + distance) % SEG) for i in range(SEG)]

    gathered = jnp.concatenate(
        [traces] + [lax.ppermute(traces, "seg", along(d)) for d in (1, 3, 2)], axis=0
    )
    blocks = order_rows(station_slot, gathered)
    mates = [(i, i ^ 1) for i in range(owners)]
    crossing = [(i, i + 1) for i in range(1, owners - 1, 2)]
    crossing += [(b, a) for a, b in crossing]
    far = lax.ppermute(blocks, pair, crossing)
    mate = lax.ppermute(blocks, pair, mates)
    own_white = whiten_own(blocks, table, window, bins)
    place = jnp.stack([lax.axis_index(pair), lax.axis_index("seg")]).astype(jnp.int32)
    meta = jnp.concatenate([block_pairs.reshape(-1), pair_count, place])
    return unpack(correlate(meta, own_white, mate, far, table, window, bins))


def solution(mesh):
    devices = mesh.devices.reshape(SEG, -1, 2)
    split = Mesh(devices, ("seg", "chip", "core"))
    pair = ("chip", "core")
    return jax.shard_map(
        body,
        mesh=split,
        in_specs=(P("seg", pair, None), P(pair, None), P(pair, None), P(pair)),
        out_specs=P(pair, None, "seg"),
        check_vma=False,
    )
```

time: 140 us -> 39 us (0.28)
  local copies, waits for them, and re-layouts: 51.6 us -> 2.32 us
  matrix products: 33.8 us -> 0 us
  other arithmetic: 29.9 us -> 2.25 us
  Pallas kernels: 0 us -> 18.1 us
  blocking collectives: 13.4 us -> 0 us
  waiting for transfers between devices: 0.01 us -> 6.66 us
    dot_general x7 -> x0, matrix products: 33.8 us -> none  [the longest x4 26.9 us: product(): jnp.einsum('szif,szjf->zfij', left_part, right_part, preferred_element_ty...]
    convert_element_type x2 -> x0, other arithmetic: 22.3 us -> none  [the longest x1 15.3 us: inverse_table(): (weight * jnp.cos(angles)).astype(jnp.bfloat16)]
    pallas_call x0 -> x3, Pallas kernels: none -> 18.1 us  [the longest x1 11.9 us: correlate(): pl.pallas_call(main_kernel, out_shape=jax.ShapeDtypeStruct((OUT_ROWS, LAN...]
    gather x4 -> x0, local copies, waits for them, and re-layouts: 16.2 us -> none  [the longest x2 8.58 us: body(): first_rows = jnp.take(candidates, first_index, axis=1)]
    all_gather x1 -> x0, blocking collectives: 13.4 us -> none  [body(): source = lax.all_gather(ordered, 'seg', axis=0, tiled=True)]
    another operation x2 -> x0, local copies, waits for them, and re-layouts: 10.4 us -> none
    dot_general x4 -> x0, local copies, waits for them, and re-layouts: 9.59 us -> none  [product(): jnp.einsum('szif,szjf->zfij', left_part, right_part, preferred_element_ty...]
    convert_element_type x1 -> x0, local copies, waits for them, and re-layouts: 8.44 us -> none  [body(): jnp.where(live_mask[:, None, None], correlated, 0.0).astype(jnp.bfloat16)]
  transfers between devices with their start and end apart: 2 -> 5, of which waited for: 0 -> 3; matrix products, arithmetic and copies ran while one was open for 13% -> 4% of each run, Pallas kernels for 0% -> 11%
where the time goes in v1:
time: 39 us; the launch traced here: 38.7 us
  Pallas kernels  18.1 us (46%)
  starting transfers between devices  8.72 us (22%)
  waiting for transfers between devices  6.66 us (17%)
  local copies, waits for them, and re-layouts  2.32 us (6%)
  other arithmetic  2.25 us (6%)
  between operations  0.67 us (2%)
    pallas_call x1, Pallas kernels, correlate(): pl.pallas_call(main_kernel, out_shape=jax.ShapeDtypeStruct((OUT_ROWS, LAN...  11.9 us
    ppermute x3, starting transfers between devices, body(): lax.ppermute(traces, 'seg', along(d))  5.05 us
    ppermute x3, waiting for transfers between devices, body(): lax.ppermute(traces, 'seg', along(d))  4.79 us
    pallas_call x1, Pallas kernels, whiten_own(): pl.pallas_call(own_kernel, out_shape=jax.ShapeDtypeStruct((2 * ROWS, 2 *...  4.27 us
    ppermute x1, starting transfers between devices, body(): far = lax.ppermute(blocks, pair, crossing)  2.5 us
    unnamed x5, local copies, waits for them, and re-layouts  2.24 us
    pallas_call x1, Pallas kernels, order_rows(): pl.pallas_call(order_kernel, out_shape=jax.ShapeDtypeStruct((2, ROWS, N),...  1.94 us
    ppermute x1, waiting for transfers between devices, body(): far = lax.ppermute(blocks, pair, crossing)  1.86 us
  transfers between devices with their start and end apart: 5, of which 3 were waited for; matrix products, arithmetic and copies ran while one was open for 4% of the time, Pallas kernels for 11%

profile of v1, /device:TPU:128, one launch (start us, length us, event | category | flops | bytes accessed | tf_op | source)
XLA Modules:
  0.0 38.7 jit_solution(1173486336898522865)
XLA Ops:
  0.0 2.8 %collective-permute-start.1 = (bf16[1,64,640]{2,1,0:T(8,128)(2,1)}, bf16[1,64,640]{2,1,0:T(8,128)(2,1)S(1)}, u32[]{:S(2)}, u32[]{:S(2)}) collective-permute-start(bf16[1,64,640]{2,1,0:T(8,128)(2,1)} %param.7), channel_id=1, source_target_pairs={{0,192},{64,0},{128,64},{192,128},{1,193},{65,1},{129,65},{193,129... | collective-permute-start | bytes 245768 | tf_op jit(solution)/shard_map/ppermute | solution.py:292
  2.8 0.0 collective-permute-start
  2.8 2.3 %collective-permute-start.2 = (bf16[1,64,640]{2,1,0:T(8,128)(2,1)}, bf16[1,64,640]{2,1,0:T(8,128)(2,1)S(1)}, u32[]{:S(2)}, u32[]{:S(2)}) collective-permute-start(bf16[1,64,640]{2,1,0:T(8,128)(2,1)} %param.7), channel_id=1, source_target_pairs={{0,128},{64,192},{128,0},{192,64},{1,129},{65,193},{129,1},{193,65... | collective-permute-start | bytes 245768 | tf_op jit(solution)/shard_map/ppermute | solution.py:292
  5.1 0.1 collective-permute-done.1
  5.1 4.7 %collective-permute-done = bf16[1,64,640]{2,1,0:T(8,128)(2,1)S(1)} collective-permute-done((bf16[1,64,640]{2,1,0:T(8,128)(2,1)}, bf16[1,64,640]{2,1,0:T(8,128)(2,1)S(1)}, u32[]{:S(2)}, u32[]{:S(2)}) %collective-permute-start) | collective-permute-done | bytes 81952 | tf_op jit(solution)/shard_map/ppermute | solution.py:292
  9.8 0.0 collective-permute-done.2
  9.8 1.7 %pad_maximum_fusion.gathered_ref = bf16[4,64,640]{2,1,0:T(8,128)(2,1)} fusion(bf16[1,64,640]{2,1,0:T(8,128)(2,1)S(1)} %collective-permute-done.2, bf16[1,64,640]{2,1,0:T(8,128)(2,1)S(1)} %collective-permute-done.1, bf16[1,64,640]{2,1,0:T(8,128)(2,1)S(1)} %collective-permute-done, bf16[1,64,640]{2,1,0:T(8,128)(2,1)} %param.7), kind=kLoop, calls=%fused_computation | loop fusion | flops 491520 | bytes 655360 | tf_op jit(solution)/shard_map/concatenate | solution.py:291
  11.5 1.9 %order_rows.1.blocks_ref = bf16[2,128,640]{2,1,0:T(8,128)(2,1)} custom-call(s32[1,64]{1,0:T(1,128)} %slot_ref.1, bf16[4,64,640]{2,1,0:T(8,128)(2,1)} %pad_maximum_fusion.gathered_ref), custom_call_target="tpu_custom_call" | custom-call | tf_op jit(solution)/shard_map/order_rows/pallas_call | solution.py:64
  13.4 2.5 %collective-permute-start.4 = (bf16[2,128,640]{2,1,0:T(8,128)(2,1)}, bf16[2,128,640]{2,1,0:T(8,128)(2,1)S(1)}, u32[]{:S(2)}, u32[]{:S(2)}) collective-permute-start(bf16[2,128,640]{2,1,0:T(8,128)(2,1)} %order_rows.1.blocks_ref), channel_id=1, source_target_pairs={{1,2},{3,4},{5,6},{7,8},{9,10},{11,12},{13,14},{15,16},{17,18},{19... | collective-permute-start | bytes 983048 | tf_op jit(solution)/shard_map/ppermute | solution.py:298
  16.0 1.2 %collective-permute-start.3 = (bf16[2,128,640]{2,1,0:T(8,128)(2,1)}, bf16[2,128,640]{2,1,0:T(8,128)(2,1)S(1)}, u32[]{:S(2)}, u32[]{:S(2)}) collective-permute-start(bf16[2,128,640]{2,1,0:T(8,128)(2,1)} %order_rows.1.blocks_ref), channel_id=1, source_target_pairs={{0,1},{1,0},{2,3},{3,2},{4,5},{5,4},{6,7},{7,6},{8,9},{9,8},{10,11... | collective-permute-start | bytes 983048 | tf_op jit(solution)/shard_map/ppermute | solution.py:299
  17.8 0.8 %copy.10 = s32[4,2]{1,0:T(4,128)S(1)} copy(s32[4,2]{0,1:T(2,128)} %param.9) | data formatting | bytes 64 | tf_op args[2]
  18.5 0.1 reshape.9
  18.6 0.6 %pad_add_fusion.meta_ref = s32[11]{0:T(128)} fusion(s32[1]{0:T(128)} %bitcast.1, s32[1]{0:T(128)} %bitcast, s32[1]{0:T(128)S(6)} %copy.12, s32[8]{0:T(128)S(1)} %reshape.9), kind=kLoop, calls=%fused_computation.1 | loop fusion | flops 33 | bytes 88 | tf_op jit(solution)/shard_map/concatenate | solution.py:302
  19.2 4.3 %whiten_own.1.own_ref = f32[256,1280]{1,0:T(8,128)} custom-call(bf16[2,128,640]{2,1,0:T(8,128)(2,1)} %order_rows.1.blocks_ref, bf16[640,1280]{1,0:T(8,128)(2,1)} %constant.22.clone.table_ref, bf16[640,640]{1,0:T(8,128)(2,1)} %constant.23.clone.window_ref, f32[2,640]{1,0:T(2,128)} %constant.24.clone.bins_ref), custom_call_target="tpu_custom_call" | custom-call | tf_op jit(solution)/shard_map/whiten_own/pallas_call | solution.py:113
  23.5 1.9 %collective-permute-done.4.far_ref = bf16[2,128,640]{2,1,0:T(8,128)(2,1)S(1)} collective-permute-done((bf16[2,128,640]{2,1,0:T(8,128)(2,1)}, bf16[2,128,640]{2,1,0:T(8,128)(2,1)S(1)}, u32[]{:S(2)}, u32[]{:S(2)}) %collective-permute-start.4) | collective-permute-done | bytes 327712 | tf_op jit(solution)/shard_map/ppermute | solution.py:298
  25.4 0.0 copy-start
  25.4 0.0 collective-permute-done.3.mate_ref
  25.4 0.7 %copy-done = bf16[2,128,640]{2,1,0:T(8,128)(2,1)} copy-done((bf16[2,128,640]{2,1,0:T(8,128)(2,1)}, bf16[2,128,640]{2,1,0:T(8,128)(2,1)S(1)}, u32[]{:S(2)}) %copy-start) | copy-done | bytes 327704
  26.1 0.0 copy-start.1
  26.1 0.7 %copy-done.1 = bf16[2,128,640]{2,1,0:T(8,128)(2,1)} copy-done((bf16[2,128,640]{2,1,0:T(8,128)(2,1)}, bf16[2,128,640]{2,1,0:T(8,128)(2,1)S(1)}, u32[]{:S(2)}) %copy-start.1) | copy-done | bytes 327704
  26.8 11.9 %correlate.1 = bf16[10248,128]{1,0:T(8,128)(2,1)} custom-call(s32[11]{0:T(128)} %pad_add_fusion.meta_ref, f32[256,1280]{1,0:T(8,128)} %whiten_own.1.own_ref, bf16[2,128,640]{2,1,0:T(8,128)(2,1)} %copy-done.1, bf16[2,128,640]{2,1,0:T(8,128)(2,1)} %copy-done, bf16[640,1280]{1,0:T(8,128)(2,1)} %constant.22.clone.table_ref, ...), custom_call_target="tpu_custom_call" | custom-call | tf_op jit(solution)/shard_map/correlate/pallas_call | solution.py:256
Async XLA Ops:
  0.0 5.1 %collective-permute-start.1 = (bf16[1,64,640]{2,1,0:T(8,128)(2,1)}, bf16[1,64,640]{2,1,0:T(8,128)(2,1)S(1)}, u32[]{:S(2)}, u32[]{:S(2)}) collective-permute-start(bf16[1,64,640]{2,1,0:T(8,128)(2,1)} %param.7), channel_id=1, source_target_pairs={{0,192},{64,0},{128,64},{192,128},{1,193},{65,1},{129,65},{193,129... | collective-permute-start | bytes 245768 | tf_op jit(solution)/shard_map/ppermute | solution.py:292
  2.8 7.1 %collective-permute-start = (bf16[1,64,640]{2,1,0:T(8,128)(2,1)}, bf16[1,64,640]{2,1,0:T(8,128)(2,1)S(1)}, u32[]{:S(2)}, u32[]{:S(2)}) collective-permute-start(bf16[1,64,640]{2,1,0:T(8,128)(2,1)} %param.7), channel_id=1, source_target_pairs={{0,64},{64,128},{128,192},{192,0},{1,65},{65,129},{129,193},{193,1... | collective-permute-start | bytes 245768 | tf_op jit(solution)/shard_map/ppermute | solution.py:292
  2.8 7.1 %collective-permute-start.2 = (bf16[1,64,640]{2,1,0:T(8,128)(2,1)}, bf16[1,64,640]{2,1,0:T(8,128)(2,1)S(1)}, u32[]{:S(2)}, u32[]{:S(2)}) collective-permute-start(bf16[1,64,640]{2,1,0:T(8,128)(2,1)} %param.7), channel_id=1, source_target_pairs={{0,128},{64,192},{128,0},{192,64},{1,129},{65,193},{129,1},{193,65... | collective-permute-start | bytes 245768 | tf_op jit(solution)/shard_map/ppermute | solution.py:292
  13.4 11.9 %collective-permute-start.4 = (bf16[2,128,640]{2,1,0:T(8,128)(2,1)}, bf16[2,128,640]{2,1,0:T(8,128)(2,1)S(1)}, u32[]{:S(2)}, u32[]{:S(2)}) collective-permute-start(bf16[2,128,640]{2,1,0:T(8,128)(2,1)} %order_rows.1.blocks_ref), channel_id=1, source_target_pairs={{1,2},{3,4},{5,6},{7,8},{9,10},{11,12},{13,14},{15,16},{17,18},{19... | collective-permute-start | bytes 983048 | tf_op jit(solution)/shard_map/ppermute | solution.py:298
  16.0 9.4 %collective-permute-start.3 = (bf16[2,128,640]{2,1,0:T(8,128)(2,1)}, bf16[2,128,640]{2,1,0:T(8,128)(2,1)S(1)}, u32[]{:S(2)}, u32[]{:S(2)}) collective-permute-start(bf16[2,128,640]{2,1,0:T(8,128)(2,1)} %order_rows.1.blocks_ref), channel_id=1, source_target_pairs={{0,1},{1,0},{2,3},{3,2},{4,5},{5,4},{6,7},{7,6},{8,9},{9,8},{10,11... | collective-permute-start | bytes 983048 | tf_op jit(solution)/shard_map/ppermute | solution.py:299
  25.4 0.7 %copy-start = (bf16[2,128,640]{2,1,0:T(8,128)(2,1)}, bf16[2,128,640]{2,1,0:T(8,128)(2,1)S(1)}, u32[]{:S(2)}) copy-start(bf16[2,128,640]{2,1,0:T(8,128)(2,1)S(1)} %collective-permute-done.4.far_ref) | copy-start | bytes 983044
  26.1 0.7 %copy-start.1 = (bf16[2,128,640]{2,1,0:T(8,128)(2,1)}, bf16[2,128,640]{2,1,0:T(8,128)(2,1)S(1)}, u32[]{:S(2)}) copy-start(bf16[2,128,640]{2,1,0:T(8,128)(2,1)S(1)} %collective-permute-done.3.mate_ref) | copy-start | bytes 983044

commit v2 on v1

--- a/solution.py
+++ b/solution.py
@@ -51,23 +51,29 @@
     return np.stack([1.0 / counts, weight]).astype(np.float32)
 
 
-def order_kernel(slot_ref, gathered_ref, blocks_ref):
+def order_kernel(slot_ref, *refs):
+    pieces, blocks_ref = refs[:SEG], refs[SEG]
     place = lax.broadcasted_iota(jnp.int32, (2 * BLK, 2 * BLK), 0)
     onehot = (place == slot_ref[...]).astype(bf16)
     for s in range(SEG):
-        rows = jnp.dot(onehot, gathered_ref[s], preferred_element_type=f32).astype(bf16)
+        rows = jnp.dot(onehot, pieces[s][0], preferred_element_type=f32).astype(bf16)
         blocks_ref[0, s * BLK : (s + 1) * BLK, :] = rows[:BLK]
         blocks_ref[1, s * BLK : (s + 1) * BLK, :] = rows[BLK:]
 
 
-def order_rows(station_slot, gathered):
+def grant(mib):
+    return pltpu.CompilerParams(vmem_limit_bytes=mib * 2**20)
+
+
+def order_rows(station_slot, pieces):
     return pl.pallas_call(
         order_kernel,
         out_shape=jax.ShapeDtypeStruct((2, ROWS, N), bf16),
-        in_specs=[VMEM, VMEM],
+        in_specs=[VMEM] * 5,
         out_specs=VMEM,
+        compiler_params=grant(4),
         name="order_rows",
-    )(station_slot, gathered)
+    )(station_slot, *pieces)
 
 
 def whiten_rows(rows, table_ref, window_ref, bins_ref, spec_ref, hi_ref, lo_ref, store):
@@ -116,6 +122,7 @@
         in_specs=[VMEM] * 4,
         out_specs=VMEM,
         scratch_shapes=whiten_scratch(),
+        compiler_params=grant(12),
         name="whiten_own",
     )(blocks, table, window, bins)
 
@@ -268,6 +275,7 @@
             pltpu.VMEM((2 * N * 8, LANES), bf16),
             pltpu.SemaphoreType.DMA((9,)),
         ],
+        compiler_params=grant(32),
         name="correlate",
     )(meta, own_white, mate, far, table, window, bins)
 
@@ -288,10 +296,8 @@
     def along(distance):
         return [(i, (i + distance) % SEG) for i in range(SEG)]
 
-    gathered = jnp.concatenate(
-        [traces] + [lax.ppermute(traces, "seg", along(d)) for d in (1, 3, 2)], axis=0
-    )
-    blocks = order_rows(station_slot, gathered)
+    pieces = [traces] + [lax.ppermute(traces, "seg", along(d)) for d in (1, 3, 2)]
+    blocks = order_rows(station_slot, pieces)
     mates = [(i, i ^ 1) for i in range(owners)]
     crossing = [(i, i + 1) for i in range(1, owners - 1, 2)]
     crossing += [(b, a) for a, b in crossing]

time: 39 us -> 33.8 us (0.87)
  Pallas kernels: 18.1 us -> 11.9 us
  local copies, waits for them, and re-layouts: 2.32 us -> 5.67 us
  other arithmetic: 2.25 us -> 0.08 us
    unnamed x5 -> x15, local copies, waits for them, and re-layouts: 2.24 us -> 5.58 us
    pallas_call x1, Pallas kernels: 4.27 us -> 1.45 us  [whiten_own(): pl.pallas_call(own_kernel, out_shape=jax.ShapeDtypeStruct((2 * ROWS, 2 *...]
    pallas_call x1, Pallas kernels: 1.94 us -> 0.22 us  [order_rows(): pl.pallas_call(order_kernel, out_shape=jax.ShapeDtypeStruct((2, ROWS, N),...]
    pallas_call x1, Pallas kernels: 11.9 us -> 10.2 us  [correlate(): pl.pallas_call(main_kernel, out_shape=jax.ShapeDtypeStruct((OUT_ROWS, LAN...]
    concatenate x1 -> x0, other arithmetic: 1.66 us -> none  [body(): jnp.concatenate([traces] + [lax.ppermute(traces, 'seg', along(d)) for d i...]
    concatenate x1, other arithmetic: 0.59 us -> 0.08 us  [body(): meta = jnp.concatenate([block_pairs.reshape(-1), pair_count, place])]
  transfers between devices with their start and end apart: 5 -> 5, of which waited for: 3 -> 3; matrix products, arithmetic and copies ran while one was open for 4% -> 3% of each run, Pallas kernels for 11% -> 4%
where the time goes in v2:
time: 33.8 us; the launch traced here: 33.5 us
  Pallas kernels  11.9 us (35%)
  starting transfers between devices  8.74 us (26%)
  waiting for transfers between devices  6.49 us (19%)
  local copies, waits for them, and re-layouts  5.67 us (17%)
  between operations  0.69 us (2%)
    pallas_call x1, Pallas kernels, correlate(): pl.pallas_call(main_kernel, out_shape=jax.ShapeDtypeStruct((OUT_ROWS, LAN...  10.2 us
    unnamed x15, local copies, waits for them, and re-layouts  5.58 us
    ppermute x3, starting transfers between devices, body(): lax.ppermute(traces, 'seg', along(d))  5.05 us
    ppermute x3, waiting for transfers between devices, body(): lax.ppermute(traces, 'seg', along(d))  4.79 us
    ppermute x1, starting transfers between devices, body(): far = lax.ppermute(blocks, pair, crossing)  2.5 us
    ppermute x1, waiting for transfers between devices, body(): far = lax.ppermute(blocks, pair, crossing)  1.7 us
    pallas_call x1, Pallas kernels, whiten_own(): pl.pallas_call(own_kernel, out_shape=jax.ShapeDtypeStruct((2 * ROWS, 2 *...  1.45 us
    ppermute x1, starting transfers between devices, body(): mate = lax.ppermute(blocks, pair, mates)  1.19 us
  transfers between devices with their start and end apart: 5, of which 3 were waited for; matrix products, arithmetic and copies ran while one was open for 3% of the time, Pallas kernels for 4%

profile of v2, /device:TPU:128, one launch (start us, length us, event | category | flops | bytes accessed | tf_op | source)
XLA Modules:
  0.0 33.5 jit_solution(552183720520234280)
XLA Ops:
  0.0 2.8 %collective-permute-start.1 = (bf16[1,64,640]{2,1,0:T(8,128)(2,1)}, bf16[1,64,640]{2,1,0:T(8,128)(2,1)S(1)}, u32[]{:S(2)}, u32[]{:S(2)}) collective-permute-start(bf16[1,64,640]{2,1,0:T(8,128)(2,1)} %refs_0_.1), channel_id=1, source_target_pairs={{0,192},{64,0},{128,64},{192,128},{1,193},{65,1},{129,65},{193,129... | collective-permute-start | bytes 245768 | tf_op jit(solution)/shard_map/ppermute | solution.py:299
  2.8 0.0 collective-permute-start
  2.8 2.3 %collective-permute-start.2 = (bf16[1,64,640]{2,1,0:T(8,128)(2,1)}, bf16[1,64,640]{2,1,0:T(8,128)(2,1)S(1)}, u32[]{:S(2)}, u32[]{:S(2)}) collective-permute-start(bf16[1,64,640]{2,1,0:T(8,128)(2,1)} %refs_0_.1), channel_id=1, source_target_pairs={{0,128},{64,192},{128,0},{192,64},{1,129},{65,193},{129,1},{193,65... | collective-permute-start | bytes 245768 | tf_op jit(solution)/shard_map/ppermute | solution.py:299
  5.1 0.1 collective-permute-done.1.refs_2_
  5.1 4.7 %collective-permute-done.refs_1_ = bf16[1,64,640]{2,1,0:T(8,128)(2,1)S(1)} collective-permute-done((bf16[1,64,640]{2,1,0:T(8,128)(2,1)}, bf16[1,64,640]{2,1,0:T(8,128)(2,1)S(1)}, u32[]{:S(2)}, u32[]{:S(2)}) %collective-permute-start) | collective-permute-done | bytes 81952 | tf_op jit(solution)/shard_map/ppermute | solution.py:299
  9.8 0.0 collective-permute-done.2.refs_3_
  9.8 0.9 %copy-done.4 = bf16[1,64,640]{2,1,0:T(8,128)(2,1)S(1)} copy-done((bf16[1,64,640]{2,1,0:T(8,128)(2,1)S(1)}, bf16[1,64,640]{2,1,0:T(8,128)(2,1)}, u32[]{:S(2)}) %copy-start.4) | copy-done | bytes 81944
  10.7 0.0 copy-start.6
  10.7 0.7 %copy-done.6 = s32[1,64]{1,0:T(1,128)S(1)} copy-done((s32[1,64]{1,0:T(1,128)S(1)}, s32[1,64]{1,0:T(1,128)}, u32[]{:S(2)}) %copy-start.6) | copy-done | bytes 280
  11.4 0.2 order_rows.1.blocks_ref
  11.6 2.5 %collective-permute-start.4 = (bf16[2,128,640]{2,1,0:T(8,128)(2,1)S(1)}, bf16[2,128,640]{2,1,0:T(8,128)(2,1)S(1)}, u32[]{:S(2)}, u32[]{:S(2)}) collective-permute-start(bf16[2,128,640]{2,1,0:T(8,128)(2,1)S(1)} %order_rows.1.blocks_ref), channel_id=1, source_target_pairs={{1,2},{3,4},{5,6},{7,8},{9,10},{11,12},{13,14},{15,16},{17,18},{19... | collective-permute-start | bytes 983048 | tf_op jit(solution)/shard_map/ppermute | solution.py:304
  14.1 1.2 %collective-permute-start.3 = (bf16[2,128,640]{2,1,0:T(8,128)(2,1)S(1)}, bf16[2,128,640]{2,1,0:T(8,128)(2,1)S(1)}, u32[]{:S(2)}, u32[]{:S(2)}) collective-permute-start(bf16[2,128,640]{2,1,0:T(8,128)(2,1)S(1)} %order_rows.1.blocks_ref), channel_id=1, source_target_pairs={{0,1},{1,0},{2,3},{3,2},{4,5},{5,4},{6,7},{7,6},{8,9},{9,8},{10,11... | collective-permute-start | bytes 983048 | tf_op jit(solution)/shard_map/ppermute | solution.py:305
  16.0 0.8 %copy.10 = s32[4,2]{1,0:T(4,128)S(1)} copy(s32[4,2]{0,1:T(2,128)} %param.9) | data formatting | bytes 64 | tf_op args[2]
  16.7 0.1 reshape.9
  16.8 0.1 pad_add_fusion.meta_ref
  16.9 1.4 %copy-done = bf16[640,1280]{1,0:T(8,128)(2,1)S(1)} copy-done((bf16[640,1280]{1,0:T(8,128)(2,1)S(1)}, bf16[640,1280]{1,0:T(8,128)(2,1)}, u32[]{:S(2)}) %copy-start) | copy-done | bytes 1638424
  18.3 1.1 %copy-done.2 = bf16[640,640]{1,0:T(8,128)(2,1)S(1)} copy-done((bf16[640,640]{1,0:T(8,128)(2,1)S(1)}, bf16[640,640]{1,0:T(8,128)(2,1)}, u32[]{:S(2)}) %copy-start.2) | copy-done | bytes 819224
  19.5 0.7 %copy-done.5 = f32[2,640]{1,0:T(2,128)S(1)} copy-done((f32[2,640]{1,0:T(2,128)S(1)}, f32[2,640]{1,0:T(2,128)}, u32[]{:S(2)}) %copy-start.5) | copy-done | bytes 5144
  20.2 1.5 %whiten_own.1.own_ref = f32[256,1280]{1,0:T(8,128)S(1)} custom-call(bf16[2,128,640]{2,1,0:T(8,128)(2,1)S(1)} %order_rows.1.blocks_ref, bf16[640,1280]{1,0:T(8,128)(2,1)S(1)} %copy-done, bf16[640,640]{1,0:T(8,128)(2,1)S(1)} %copy-done.2, f32[2,640]{1,0:T(2,128)S(1)} %copy-done.5), custom_call_target="tpu_custom_call" | custom-call | tf_op jit(solution)/shard_map/whiten_own/pallas_call | solution.py:119
  21.6 1.7 %collective-permute-done.4.far_ref = bf16[2,128,640]{2,1,0:T(8,128)(2,1)S(1)} collective-permute-done((bf16[2,128,640]{2,1,0:T(8,128)(2,1)S(1)}, bf16[2,128,640]{2,1,0:T(8,128)(2,1)S(1)}, u32[]{:S(2)}, u32[]{:S(2)}) %collective-permute-start.4) | collective-permute-done | bytes 327712 | tf_op jit(solution)/shard_map/ppermute | solution.py:304
  23.3 0.0 collective-permute-done.3.mate_ref
  23.3 0.0 copy-done.1
  23.3 0.0 copy-done.3
  23.3 10.2 %correlate.1 = bf16[10248,128]{1,0:T(8,128)(2,1)} custom-call(s32[11]{0:T(128)S(1)} %pad_add_fusion.meta_ref, f32[256,1280]{1,0:T(8,128)S(1)} %whiten_own.1.own_ref, bf16[2,128,640]{2,1,0:T(8,128)(2,1)S(1)} %collective-permute-done.3.mate_ref, bf16[2,128,640]{2,1,0:T(8,128)(2,1)S(1)} %collective-permute-done.4.far_ref, bf16[640,1280]{1,0:T(8,128)(2,1)S(1)} %copy-done.1, ...), custom_call_target="tpu_custom_call" | custom-call | tf_op jit(solution)/shard_map/correlate/pallas_call | solution.py:263
  (6 shorter events, 0.0 us)
Async XLA Ops:
  0.0 5.1 %collective-permute-start.1 = (bf16[1,64,640]{2,1,0:T(8,128)(2,1)}, bf16[1,64,640]{2,1,0:T(8,128)(2,1)S(1)}, u32[]{:S(2)}, u32[]{:S(2)}) collective-permute-start(bf16[1,64,640]{2,1,0:T(8,128)(2,1)} %refs_0_.1), channel_id=1, source_target_pairs={{0,192},{64,0},{128,64},{192,128},{1,193},{65,1},{129,65},{193,129... | collective-permute-start | bytes 245768 | tf_op jit(solution)/shard_map/ppermute | solution.py:299
  2.8 7.1 %collective-permute-start = (bf16[1,64,640]{2,1,0:T(8,128)(2,1)}, bf16[1,64,640]{2,1,0:T(8,128)(2,1)S(1)}, u32[]{:S(2)}, u32[]{:S(2)}) collective-permute-start(bf16[1,64,640]{2,1,0:T(8,128)(2,1)} %refs_0_.1), channel_id=1, source_target_pairs={{0,64},{64,128},{128,192},{192,0},{1,65},{65,129},{129,193},{193,1... | collective-permute-start | bytes 245768 | tf_op jit(solution)/shard_map/ppermute | solution.py:299
  2.8 7.1 %collective-permute-start.2 = (bf16[1,64,640]{2,1,0:T(8,128)(2,1)}, bf16[1,64,640]{2,1,0:T(8,128)(2,1)S(1)}, u32[]{:S(2)}, u32[]{:S(2)}) collective-permute-start(bf16[1,64,640]{2,1,0:T(8,128)(2,1)} %refs_0_.1), channel_id=1, source_target_pairs={{0,128},{64,192},{128,0},{192,64},{1,129},{65,193},{129,1},{193,65... | collective-permute-start | bytes 245768 | tf_op jit(solution)/shard_map/ppermute | solution.py:299
  9.8 0.9 %copy-start.4 = (bf16[1,64,640]{2,1,0:T(8,128)(2,1)S(1)}, bf16[1,64,640]{2,1,0:T(8,128)(2,1)}, u32[]{:S(2)}) copy-start(bf16[1,64,640]{2,1,0:T(8,128)(2,1)} %refs_0_.1) | copy-start | bytes 245764
  10.7 0.7 %copy-start.6 = (s32[1,64]{1,0:T(1,128)S(1)}, s32[1,64]{1,0:T(1,128)}, u32[]{:S(2)}) copy-start(s32[1,64]{1,0:T(1,128)} %slot_ref.1) | copy-start | bytes 772
  11.6 11.7 %collective-permute-start.4 = (bf16[2,128,640]{2,1,0:T(8,128)(2,1)S(1)}, bf16[2,128,640]{2,1,0:T(8,128)(2,1)S(1)}, u32[]{:S(2)}, u32[]{:S(2)}) collective-permute-start(bf16[2,128,640]{2,1,0:T(8,128)(2,1)S(1)} %order_rows.1.blocks_ref), channel_id=1, source_target_pairs={{1,2},{3,4},{5,6},{7,8},{9,10},{11,12},{13,14},{15,16},{17,18},{19... | collective-permute-start | bytes 983048 | tf_op jit(solution)/shard_map/ppermute | solution.py:304
  14.1 9.2 %collective-permute-start.3 = (bf16[2,128,640]{2,1,0:T(8,128)(2,1)S(1)}, bf16[2,128,640]{2,1,0:T(8,128)(2,1)S(1)}, u32[]{:S(2)}, u32[]{:S(2)}) collective-permute-start(bf16[2,128,640]{2,1,0:T(8,128)(2,1)S(1)} %order_rows.1.blocks_ref), channel_id=1, source_target_pairs={{0,1},{1,0},{2,3},{3,2},{4,5},{5,4},{6,7},{7,6},{8,9},{9,8},{10,11... | collective-permute-start | bytes 983048 | tf_op jit(solution)/shard_map/ppermute | solution.py:305
  16.9 1.4 %copy-start = (bf16[640,1280]{1,0:T(8,128)(2,1)S(1)}, bf16[640,1280]{1,0:T(8,128)(2,1)}, u32[]{:S(2)}) copy-start(bf16[640,1280]{1,0:T(8,128)(2,1)} %constant.22.clone.table_ref) | copy-start | bytes 4915204
  18.3 1.1 %copy-start.2 = (bf16[640,640]{1,0:T(8,128)(2,1)S(1)}, bf16[640,640]{1,0:T(8,128)(2,1)}, u32[]{:S(2)}) copy-start(bf16[640,640]{1,0:T(8,128)(2,1)} %constant.23.clone.window_ref) | copy-start | bytes 2457604
  19.5 0.7 %copy-start.5 = (f32[2,640]{1,0:T(2,128)S(1)}, f32[2,640]{1,0:T(2,128)}, u32[]{:S(2)}) copy-start(f32[2,640]{1,0:T(2,128)} %constant.24.clone.bins_ref) | copy-start | bytes 15364
  20.2 3.2 %copy-start.1 = (bf16[640,1280]{1,0:T(8,128)(2,1)S(1)}, bf16[640,1280]{1,0:T(8,128)(2,1)}, u32[]{:S(2)}) copy-start(bf16[640,1280]{1,0:T(8,128)(2,1)} %constant.22.clone.table_ref) | copy-start | bytes 4915204
  20.2 3.2 %copy-start.3 = (bf16[640,640]{1,0:T(8,128)(2,1)S(1)}, bf16[640,640]{1,0:T(8,128)(2,1)}, u32[]{:S(2)}) copy-start(bf16[640,640]{1,0:T(8,128)(2,1)} %constant.23.clone.window_ref) | copy-start | bytes 2457604
